TPU v7x, 256 devices: a whole 4x4x8 slice. The times are simulated.
256 devices in a mesh: dp: 2 (over x_lo), expert: 8 (over z), shard: 16 (over x_hi, y, core).
Axes of the slice: x: 4 (x_hi: 2, x_lo: 2; x = x_hi * 2 + x_lo), y: 4, z: 8, core: 2. Of those that a mesh axis runs over, the one named last changes fastest.
Arguments:
- tokens: bfloat16 [2048, 6144], P(('dp', 'expert', 'shard')), may hold values from -6 to 6
- gate_up_weight: bfloat16 [8, 2, 8192, 6144], P(None, None, ('dp', 'expert', 'shard')), may hold values from -0.078125 to 0.078125
- down_weight: bfloat16 [8, 8192, 6144], P(None, ('dp', 'expert', 'shard')), may hold values from -0.0625 to 0.0625
- expert_ids: int32 [2048, 2], P(('dp', 'expert', 'shard')), may hold values from 0 to 7, as said below
- slot_ids: int32 [2048, 2], P(('dp', 'expert', 'shard')), may hold values from 0 to 3, as said below
- gate_values: float32 [2048, 2], P(('dp', 'expert', 'shard')), may hold values from 0.1 to 1
- old_place: int32 [8], replicated, may hold values from 0 to 7, each once
- new_place: int32 [8], replicated, may hold values from 0 to 7, each once
Outputs:
- mixed_out: bfloat16 [2048, 6144], P(('dp', 'expert', 'shard'))
Inputs may be any that keep to these rules, and one draw needn't show every extreme that they name: `expert_ids`: each token names 2 different experts; among the 8 tokens of one block no expert is named more than 4 times, and one expert is named exactly 4 times in every block. `slot_ids`: within one block, two choices that name the same expert have different slots. `old_place`: each expert number appears once. `new_place`: each expert number appears once.
All inputs are finite; a program needn't handle non-finite values.
Results may differ from a plain program's by a relative error of at most 0.02.
Values may be sent and summed in bfloat16 or wider, within the bound.
A program may use at most 128 MiB of HBM per device.

v0:
```python
import jax
import jax.numpy as jnp
from jax import lax
from jax.sharding import PartitionSpec as P


def placement_order(old_place, new_place):
    slot_total = old_place.shape[0]
    matches = (new_place[:, None] == old_place[None, :]).astype(jnp.int32)
    return jnp.sum(matches * jnp.arange(slot_total, dtype=jnp.int32)[None, :], axis=1)


def swiglu_rows(row_block, pair_weight):
    gate_up = jnp.einsum("rd,gud->rgu", row_block, pair_weight, preferred_element_type=jnp.float32)
    return (jax.nn.silu(gate_up[:, 0]) * gate_up[:, 1]).astype(jnp.bfloat16)


def local(
    tokens, gate_up_weight, down_weight, expert_ids, slot_ids, gate_values, old_place, new_place
):
    experts = gate_up_weight.shape[0]
    sliver = gate_up_weight.shape[2]
    model_width = tokens.shape[1]
    tok_rows = tokens.shape[0]
    choices_per_token = expert_ids.shape[1]
    capacity = 2 * tok_rows * choices_per_token // experts
    cell_count = experts * capacity
    data_ways = lax.axis_size("dp")
    slot_order = placement_order(old_place, new_place)
    cell_ids = expert_ids * capacity + slot_ids
    cell_range = jnp.arange(cell_count, dtype=jnp.int32)
    cell_hits = (cell_ids[:, :, None] == cell_range[None, None, :]).astype(jnp.float32)
    token_picks = jnp.sum(cell_hits, axis=1)
    dispatched = jnp.dot(
        token_picks.T.astype(jnp.bfloat16), tokens, preferred_element_type=jnp.float32
    ).astype(jnp.bfloat16)
    received = lax.all_to_all(
        dispatched.reshape(experts, capacity, model_width),
        "expert",
        split_axis=0,
        concat_axis=0,
        tiled=True,
    )
    own_rows = received.reshape(cell_count, model_width)
    sectioned_in = gate_up_weight.reshape(experts, 2, data_ways, sliver // data_ways, model_width)
    sectioned_down = down_weight.reshape(experts, 1, data_ways, sliver // data_ways, model_width)
    sectioned_in = jnp.take(sectioned_in, slot_order, axis=0)
    sectioned_down = jnp.take(sectioned_down, slot_order, axis=0)
    relaid_in, relaid_down = (
        lax.all_to_all(
            lax.all_to_all(sectioned_in, "dp", split_axis=2, concat_axis=3, tiled=True),
            "expert",
            split_axis=0,
            concat_axis=3,
            tiled=True,
        ),
        lax.all_to_all(
            lax.all_to_all(sectioned_down, "dp", split_axis=2, concat_axis=3, tiled=True),
            "expert",
            split_axis=0,
            concat_axis=3,
            tiled=True,
        ),
    )
    full_in, full_down = (
        lax.all_gather(relaid_in, "dp", axis=3, tiled=True),
        lax.all_gather(relaid_down, "dp", axis=3, tiled=True),
    )
    pair_in = full_in.reshape(2, -1, model_width)
    pair_down = full_down.reshape(-1, model_width)
    group_rows = lax.all_gather(own_rows, "shard", axis=0, tiled=True)
    summed = lax.psum_scatter(
        jnp.dot(
            swiglu_rows(group_rows, pair_in), pair_down, preferred_element_type=jnp.float32
        ).astype(jnp.bfloat16),
        "shard",
        scatter_dimension=0,
        tiled=True,
    )
    returned = lax.all_to_all(
        summed.reshape(experts, capacity, model_width),
        "expert",
        split_axis=0,
        concat_axis=0,
        tiled=True,
    )
    combine_weights = jnp.sum(cell_hits * gate_values[:, :, None], axis=1)
    mixed_out = jnp.dot(
        combine_weights,
        returned.reshape(cell_count, model_width).astype(jnp.float32),
        precision=lax.Precision.HIGHEST,
    )
    return mixed_out.astype(jnp.bfloat16)


def solution(mesh):
    in_specs = (
        P(("dp", "expert", "shard"), None),
        P(None, None, ("dp", "expert", "shard"), None),
        P(None, ("dp", "expert", "shard"), None),
        P(("dp", "expert", "shard"), None),
        P(("dp", "expert", "shard"), None),
        P(("dp", "expert", "shard"), None),
        P(),
        P(),
    )
    out_specs = P(("dp", "expert", "shard"), None)
    return jax.shard_map(local, mesh=mesh, in_specs=in_specs, out_specs=out_specs, check_vma=False)
```

profile of v0, /device:TPU:8, one launch (start us, length us, event | category | flops | bytes accessed | tf_op | source)
XLA Modules:
  0.0 681.6 jit_solution(10519561180992360223)
XLA Ops:
  8.3 1.2 convolution_convert_fusion.1
  9.5 0.9 reshape.64
  10.4 8.5 %all-to-all-start = ((bf16[8,4,6144]{2,1,0:T(4,128)(2,1)}), bf16[8,4,6144]{2,1,0:T(4,128)(2,1)S(1)}, u32[]{:S(2)}, u32[]{:S(2)}) async-start(bf16[8,4,6144]{2,1,0:T(4,128)(2,1)} %reshape.64), calls=%async_computation | async-start | bytes 786432 | tf_op jit(solution)/shard_map/all_to_all | solution.py:37
  19.7 6.4 gather_fusion
  26.1 3.5 broadcast_select_fusion
  29.6 3.1 copy.24
  33.5 6.3 all-to-all-start.1
  40.8 89.5 %all-to-all-done.1 = bf16[8,2,2,16,6144]{4,3,1,0,2:T(8,128)(2,1)} async-done(((bf16[8,2,2,16,6144]{4,3,1,0,2:T(8,128)(2,1)}), bf16[8,2,2,16,6144]{4,3,1,0,2:T(8,128)(2,1)}, u32[]{:S(2)}, u32[]{:S(2)}) %all-to-all-start.1) | async-done | bytes 6291488 | tf_op jit(solution)/shard_map/all_to_all | solution.py:51
  130.3 3.5 copy.25
  133.8 145.8 %all_to_all.64 = bf16[8,2,1,32,6144]{4,3,1,2,0:T(8,128)(2,1)S(1)} all-to-all(bf16[8,2,1,32,6144]{4,3,1,2,0:T(8,128)(2,1)S(1)} %bitcast.37), channel_id=1, replica_groups=mesh['dp'=2,'expert'=8,'shard'=16] {'expert'}, dimensions={0} | all-to-all | bytes 12582912 | tf_op jit(solution)/shard_map/all_to_all | solution.py:50
  279.7 3.1 copy.27
  282.8 2.4 gather_fusion.1
  285.3 2.3 bitcast_select_fusion
  287.9 63.1 %all_to_all.65 = bf16[8,1,2,16,6144]{4,3,0,1,2:T(8,128)(2,1)S(1)} all-to-all(bf16[8,1,2,16,6144]{4,3,0,1,2:T(8,128)(2,1)S(1)} %copy.28), channel_id=1, replica_groups=mesh['dp'=2,'expert'=8,'shard'=16] {'dp'}, dimensions={2} | all-to-all | bytes 6291456 | tf_op jit(solution)/shard_map/all_to_all | solution.py:58
  351.2 66.1 %all_to_all.66 = bf16[8,1,1,32,6144]{4,3,2,1,0:T(8,128)(2,1)} all-to-all(bf16[8,1,1,32,6144]{4,3,2,1,0:T(8,128)(2,1)S(1)} %bitcast.40), channel_id=1, replica_groups=mesh['dp'=2,'expert'=8,'shard'=16] {'expert'}, dimensions={0} | all-to-all | bytes 6291456 | tf_op jit(solution)/shard_map/all_to_all | solution.py:57
  417.5 41.2 %all-gather.6.cloned.1.call-done = bf16[1,2,1,512,6144]{4,3,1,2,0:T(8,128)(2,1)} async-done(((bf16[1,2,1,256,6144]{4,3,1,2,0:T(8,128)(2,1)}), bf16[1,2,1,512,6144]{4,3,1,2,0:T(8,128)(2,1)}) %all-gather.6.cloned.1.call-update) | async-done | bytes 12582928 | tf_op jit(solution)/shard_map/all_gather | solution.py:66
  458.6 12.5 %fusion = f32[512,2,512]{2,0,1:T(8,128)} fusion(bf16[1,2,1,512,6144]{4,3,1,2,0:T(8,128)(2,1)} %all-gather.6.cloned.1.call-done, bf16[512,6144]{1,0:T(8,128)(2,1)} %all-gather.4.cloned.1.call-done), kind=kOutput, calls=%fused_computation.2 | convolution fusion | flops 6442450944 | bytes 20971520 | tf_op jit(solution)/shard_map/rd,gud->rgu/dot_general | solution.py:14
  471.2 72.6 %all-gather.8.cloned.1.call-done = bf16[1,1,1,512,6144]{4,3,2,1,0:T(8,128)(2,1)} async-done(((bf16[1,1,1,256,6144]{4,3,2,1,0:T(8,128)(2,1)}), bf16[1,1,1,512,6144]{4,3,2,1,0:T(8,128)(2,1)}) %all-gather.8.cloned.1.call-update) | async-done | bytes 6291472 | tf_op jit(solution)/shard_map/all_gather | solution.py:67
  543.8 9.7 %convolution_convert_fusion = bf16[512,6144]{1,0:T(8,128)(2,1)} fusion(bf16[1,1,1,512,6144]{4,3,2,1,0:T(8,128)(2,1)} %all-gather.8.cloned.1.call-done, f32[512,2,512]{2,0,1:T(8,128)} %fusion), kind=kOutput, calls=%fused_computation.4 | convolution fusion | flops 3225944064 | bytes 14680064 | tf_op jit(solution)/shard_map/dot_general | solution.py:73
  553.6 98.3 %reduce-scatter.2.cloned.1.call-done = bf16[32,6144]{1,0:T(8,128)(2,1)} async-done(((bf16[512,6144]{1,0:T(8,128)(2,1)}), bf16[32,6144]{1,0:T(8,128)(2,1)}) %reduce-scatter.2.cloned.1.call-update) | async-done | bytes 393232 | tf_op jit(solution)/shard_map/reduce_scatter | solution.py:72
  651.9 1.1 reshape.70
  653.0 20.0 %all_to_all.67 = bf16[8,4,6144]{2,1,0:T(4,128)(2,1)} all-to-all(bf16[8,4,6144]{2,1,0:T(4,128)(2,1)S(1)} %reshape.70), channel_id=1, replica_groups=mesh['dp'=2,'expert'=8,'shard'=16] {'expert'}, dimensions={0} | all-to-all | bytes 786432 | tf_op jit(solution)/shard_map/all_to_all | solution.py:80
  673.1 1.1 reshape.71
  674.1 0.9 convolution_convert_fusion.2
  (23 shorter events, 5.2 us)
Async XLA Ops:
  6.5 276.3 %copy-start = (bf16[8,32,6144]{2,1,0:T(8,128)(2,1)S(1)}, bf16[8,32,6144]{2,1,0:T(8,128)(2,1)}, u32[]{:S(2)}) copy-start(bf16[8,32,6144]{2,1,0:T(8,128)(2,1)} %param.10) | copy-start | bytes 9437188
  10.4 23.2 %all-to-all-start = ((bf16[8,4,6144]{2,1,0:T(4,128)(2,1)}), bf16[8,4,6144]{2,1,0:T(4,128)(2,1)S(1)}, u32[]{:S(2)}, u32[]{:S(2)}) async-start(bf16[8,4,6144]{2,1,0:T(4,128)(2,1)} %reshape.64), calls=%async_computation | async-start | bytes 786432 | tf_op jit(solution)/shard_map/all_to_all | solution.py:37
  33.5 96.8 %all-to-all-start.1 = ((bf16[8,2,2,16,6144]{4,3,1,0,2:T(8,128)(2,1)}), bf16[8,2,2,16,6144]{4,3,1,0,2:T(8,128)(2,1)}, u32[]{:S(2)}, u32[]{:S(2)}) async-start(bf16[8,2,2,16,6144]{4,3,1,0,2:T(8,128)(2,1)} %copy.24), calls=%async_computation.1 | async-start | bytes 12582912 | tf_op jit(solution)/shard_map/all_to_all | solution.py:51
  39.8 377.6 %all-gather.4.cloned.1.call-start = ((), (), s32[]{:S(2)}) async-start(), calls=%async_computation.7 | async-start | bytes 6684672 | tf_op jit(solution)/shard_map/all_gather | solution.py:71
  40.8 417.9 %all-gather.6.cloned.1.call-start = ((), (), s32[]{:S(2)}) async-start(), calls=%async_computation.8 | async-start | bytes 18874368 | tf_op jit(solution)/shard_map/all_gather | solution.py:66
  282.8 261.0 %all-gather.8.cloned.1.call-start = ((), (), s32[]{:S(2)}) async-start(), calls=%async_computation.9 | async-start | bytes 9437184 | tf_op jit(solution)/shard_map/all_gather | solution.py:67
  417.4 234.5 %reduce-scatter.2.cloned.1.call-start = ((), (), s32[]{:S(2)}) async-start(), calls=%async_computation.10 | async-start | bytes 6684672 | tf_op jit(solution)/shard_map/reduce_scatter | solution.py:72
  543.8 131.2 %copy-start.1 = (bf16[8,32,6144]{2,1,0:T(8,128)(2,1)S(1)}, bf16[8,32,6144]{2,1,0:T(8,128)(2,1)}, u32[]{:S(2)}) copy-start(bf16[8,32,6144]{2,1,0:T(8,128)(2,1)} %param.10) | copy-start | bytes 9437188
Sparse Core Ops, SparseCore 0:
  43.4 90.1 all-gather.3
  282.9 175.6 all-gather.5
  460.4 83.3 all-gather.7
  553.7 98.1 reduce-scatter.1
where the time goes:
time: 682 us
  waiting for transfers between devices  303 us (44%)
  blocking collectives  295 us (43%)
  matrix products  24.3 us (4%)
  local copies, waits for them, and re-layouts  23.1 us (3%)
  starting transfers between devices  15 us (2%)
  between operations  13.2 us (2%)
  other arithmetic  8.31 us (1%)
    all_to_all x1, blocking collectives, local(): lax.all_to_all(lax.all_to_all(sectioned_in, 'dp', split_axis=2, concat_ax...  146 us
    reduce_scatter x1, waiting for transfers between devices, local(): lax.psum_scatter(jnp.dot(swiglu_rows(group_rows, pair_in), pair_down, pre...  98.3 us
    all_to_all x1, waiting for transfers between devices, local(): lax.all_to_all(sectioned_in, 'dp', split_axis=2, concat_axis=3, tiled=True)  89.5 us
    all_gather x1, waiting for transfers between devices, local(): lax.all_gather(relaid_down, 'dp', axis=3, tiled=True)  72.6 us
    all_to_all x1, blocking collectives, local(): lax.all_to_all(lax.all_to_all(sectioned_down, 'dp', split_axis=2, concat_...  66.1 us
    all_to_all x1, blocking collectives, local(): lax.all_to_all(sectioned_down, 'dp', split_axis=2, concat_axis=3, tiled=T...  63.1 us
    all_gather x1, waiting for transfers between devices, local(): lax.all_gather(relaid_in, 'dp', axis=3, tiled=True)  41.2 us
    all_to_all x1, blocking collectives, local(): lax.all_to_all(summed.reshape(experts, capacity, model_width), 'expert',...  20 us
  transfers between devices with their start and end apart: 6, of which 5 were waited for; matrix products, arithmetic and copies ran while one was open for 6% of the time, Pallas kernels for 0%

commit v1 on v0

--- a/solution.py
+++ b/solution.py
@@ -2,6 +2,15 @@
 import jax.numpy as jnp
 from jax import lax
 from jax.sharding import PartitionSpec as P
+
+
+def group_the_cubes(array_in, chip_axis):
+    return jnp.concatenate(
+        lax.all_to_all(
+            jnp.stack(jnp.split(array_in, lax.axis_size(chip_axis), 0)), chip_axis, 0, 0
+        ),
+        3,
+    )
 
 
 def placement_order(old_place, new_place):
@@ -54,12 +63,8 @@
             concat_axis=3,
             tiled=True,
         ),
-        lax.all_to_all(
-            lax.all_to_all(sectioned_down, "dp", split_axis=2, concat_axis=3, tiled=True),
-            "expert",
-            split_axis=0,
-            concat_axis=3,
-            tiled=True,
+        group_the_cubes(
+            lax.all_to_all(sectioned_down, "dp", split_axis=2, concat_axis=3, tiled=True), "expert"
         ),
     )
     full_in, full_down = (

time: 682 us -> 659 us (0.966)
  blocking collectives: 295 us -> 94.4 us
  waiting for transfers between devices: 303 us -> 467 us
  starting transfers between devices: 15 us -> 23.8 us
  local copies, waits for them, and re-layouts: 23.1 us -> 30.8 us
    all_to_all x3 -> x1, blocking collectives: 275 us -> 74.5 us  [group_the_cubes(): lax.all_to_all(jnp.stack(jnp.split(array_in, lax.axis_size(chip_axis), 0)...]
    all_to_all x0 -> x2, waiting for transfers between devices: none -> 174 us  [the longest x1 131 us: local(): lax.all_to_all(lax.all_to_all(sectioned_in, 'dp', split_axis=2, concat_ax...]
    all_to_all x1, waiting for transfers between devices: 89.5 us -> 67.9 us  [local(): lax.all_to_all(sectioned_in, 'dp', split_axis=2, concat_axis=3, tiled=True)]
    all_to_all x0 -> x2, starting transfers between devices: none -> 8.71 us  [the longest x1 4.77 us: local(): lax.all_to_all(lax.all_to_all(sectioned_in, 'dp', split_axis=2, concat_ax...]
  transfers between devices with their start and end apart: 6 -> 8, of which waited for: 5 -> 7; matrix products, arithmetic and copies ran while one was open for 6% -> 5% of each run, Pallas kernels for 0% -> 0%
where the time goes in v1:
time: 659 us; the launch traced here: 658 us
  waiting for transfers between devices  467 us (71%)
  blocking collectives  94.4 us (14%)
  local copies, waits for them, and re-layouts  30.8 us (5%)
  starting transfers between devices  23.8 us (4%)
  matrix products  21.8 us (3%)
  between operations  13.3 us (2%)
  other arithmetic  6.81 us (1%)
    all_to_all x1, waiting for transfers between devices, local(): lax.all_to_all(lax.all_to_all(sectioned_in, 'dp', split_axis=2, concat_ax...  131 us
    reduce_scatter x1, waiting for transfers between devices, local(): lax.psum_scatter(jnp.dot(swiglu_rows(group_rows, pair_in), pair_down, pre...  98.4 us
    all_to_all x1, blocking collectives, group_the_cubes(): lax.all_to_all(jnp.stack(jnp.split(array_in, lax.axis_size(chip_axis), 0)...  74.5 us
    all_gather x1, waiting for transfers between devices, local(): lax.all_gather(relaid_down, 'dp', axis=3, tiled=True)  71.9 us
    all_to_all x1, waiting for transfers between devices, local(): lax.all_to_all(sectioned_in, 'dp', split_axis=2, concat_axis=3, tiled=True)  67.9 us
    all_gather x1, waiting for transfers between devices, local(): lax.all_gather(relaid_in, 'dp', axis=3, tiled=True)  47.3 us
    all_to_all x1, waiting for transfers between devices, local(): lax.all_to_all(sectioned_down, 'dp', split_axis=2, concat_axis=3, tiled=T...  42.8 us
    all_to_all x1, blocking collectives, local(): lax.all_to_all(summed.reshape(experts, capacity, model_width), 'expert',...  20 us
  transfers between devices with their start and end apart: 8, of which 7 were waited for; matrix products, arithmetic and copies ran while one was open for 5% of the time, Pallas kernels for 0%

profile of v1, /device:TPU:8, one launch (start us, length us, event | category | flops | bytes accessed | tf_op | source)
XLA Modules:
  0.0 658.4 jit_solution(901327273945168936)
XLA Ops:
  7.6 6.4 gather_fusion
  14.0 3.5 broadcast_select_fusion
  17.4 3.1 copy.22
  20.5 6.5 all-to-all-start.1
  27.1 1.2 convolution_convert_fusion.1
  29.2 67.9 %all-to-all-done.1 = bf16[8,2,2,16,6144]{4,3,1,0,2:T(8,128)(2,1)} async-done(((bf16[8,2,2,16,6144]{4,3,1,0,2:T(8,128)(2,1)}), bf16[8,2,2,16,6144]{4,3,1,0,2:T(8,128)(2,1)}, u32[]{:S(2)}, u32[]{:S(2)}) %all-to-all-start.1) | async-done | bytes 6291488 | tf_op jit(solution)/shard_map/all_to_all | solution.py:60
  97.1 8.5 %all-to-all-start = ((bf16[8,4,6144]{2,1,0:T(4,128)(2,1)}), bf16[8,4,6144]{2,1,0:T(4,128)(2,1)S(1)}, u32[]{:S(2)}, u32[]{:S(2)}) async-start(bf16[8,4,6144]{2,1,0:T(4,128)(2,1)} %reshape.82), calls=%async_computation | async-start | bytes 786432 | tf_op jit(solution)/shard_map/all_to_all | solution.py:46
  105.6 6.2 copy.23
  111.8 7.6 %all-to-all-done = bf16[8,4,6144]{2,1,0:T(4,128)(2,1)S(1)} async-done(((bf16[8,4,6144]{2,1,0:T(4,128)(2,1)}), bf16[8,4,6144]{2,1,0:T(4,128)(2,1)S(1)}, u32[]{:S(2)}, u32[]{:S(2)}) %all-to-all-start) | async-done | bytes 393248 | tf_op jit(solution)/shard_map/all_to_all | solution.py:46
  119.4 4.8 all-to-all-start.2
  125.1 2.4 gather_fusion.1
  127.6 2.3 bitcast_select_fusion
  129.8 2.0 copy.26
  131.8 131.4 %all-to-all-done.2 = bf16[8,2,1,32,6144]{4,3,1,2,0:T(8,128)(2,1)} async-done(((bf16[8,2,1,32,6144]{4,3,1,2,0:T(8,128)(2,1)}), bf16[8,2,1,32,6144]{4,3,1,2,0:T(8,128)(2,1)}, u32[]{:S(2)}, u32[]{:S(2)}) %all-to-all-start.2) | async-done | bytes 6291488 | tf_op jit(solution)/shard_map/all_to_all | solution.py:59
  263.3 3.9 all-to-all-start.3
  267.3 6.2 copy.25
  273.6 42.8 %all-to-all-done.3 = bf16[8,1,2,16,6144]{4,3,0,1,2:T(8,128)(2,1)S(1)} async-done(((bf16[8,1,2,16,6144]{4,3,0,1,2:T(8,128)(2,1)}), bf16[8,1,2,16,6144]{4,3,0,1,2:T(8,128)(2,1)S(1)}, u32[]{:S(2)}, u32[]{:S(2)}) %all-to-all-start.3) | async-done | bytes 3145760 | tf_op jit(solution)/shard_map/all_to_all | solution.py:67
  316.9 74.5 %all_to_all.54 = bf16[8,1,1,1,32,6144]{5,4,3,2,1,0:T(8,128)(2,1)} all-to-all(bf16[8,1,1,1,32,6144]{5,4,3,2,1,0:T(8,128)(2,1)S(1)} %constant_dynamic-update-slice_fusion), channel_id=1, replica_groups=mesh['dp'=2,'expert'=8,'shard'=16] {'expert'}, dimensions={0} | all-to-all | bytes 6291456 | tf_op jit(solution)/shard_map/all_to_all | solution.py:9
  391.4 47.3 %all-gather.6.cloned.1.call-done = bf16[1,2,1,512,6144]{4,3,1,2,0:T(8,128)(2,1)} async-done(((bf16[1,2,1,256,6144]{4,3,1,2,0:T(8,128)(2,1)}), bf16[1,2,1,512,6144]{4,3,1,2,0:T(8,128)(2,1)}) %all-gather.6.cloned.1.call-update) | async-done | bytes 12582928 | tf_op jit(solution)/shard_map/all_gather | solution.py:71
  438.7 11.6 %fusion = f32[512,2,512]{2,0,1:T(8,128)S(1)} fusion(bf16[1,2,1,512,6144]{4,3,1,2,0:T(8,128)(2,1)} %all-gather.6.cloned.1.call-done, bf16[512,6144]{1,0:T(8,128)(2,1)} %all-gather.4.cloned.1.call-done), kind=kOutput, calls=%fused_computation.2 | convolution fusion | flops 6442450944 | bytes 20971520 | tf_op jit(solution)/shard_map/rd,gud->rgu/dot_general | solution.py:23
  450.3 71.9 %all-gather.8.cloned.1.call-done = bf16[1,1,1,512,6144]{4,3,2,1,0:T(8,128)(2,1)} async-done(((bf16[1,1,1,256,6144]{4,3,2,1,0:T(8,128)(2,1)}), bf16[1,1,1,512,6144]{4,3,2,1,0:T(8,128)(2,1)}) %all-gather.8.cloned.1.call-update) | async-done | bytes 6291472 | tf_op jit(solution)/shard_map/all_gather | solution.py:72
  522.2 8.1 %convolution_convert_fusion = bf16[512,6144]{1,0:T(8,128)(2,1)} fusion(bf16[1,1,1,512,6144]{4,3,2,1,0:T(8,128)(2,1)} %all-gather.8.cloned.1.call-done, f32[512,2,512]{2,0,1:T(8,128)S(1)} %fusion), kind=kOutput, calls=%fused_computation.4 | convolution fusion | flops 3225944064 | bytes 14680064 | tf_op jit(solution)/shard_map/dot_general | solution.py:78
  530.4 98.4 %reduce-scatter.2.cloned.1.call-done = bf16[32,6144]{1,0:T(8,128)(2,1)} async-done(((bf16[512,6144]{1,0:T(8,128)(2,1)}), bf16[32,6144]{1,0:T(8,128)(2,1)}) %reduce-scatter.2.cloned.1.call-update) | async-done | bytes 393232 | tf_op jit(solution)/shard_map/reduce_scatter | solution.py:77
  629.9 20.0 %all_to_all.55 = bf16[8,4,6144]{2,1,0:T(4,128)(2,1)} all-to-all(bf16[8,4,6144]{2,1,0:T(4,128)(2,1)S(1)} %reshape.89), channel_id=1, replica_groups=mesh['dp'=2,'expert'=8,'shard'=16] {'expert'}, dimensions={0} | all-to-all | bytes 786432 | tf_op jit(solution)/shard_map/all_to_all | solution.py:85
  (39 shorter events, 6.7 us)
Async XLA Ops:
  6.5 118.6 %copy-start = (bf16[8,32,6144]{2,1,0:T(8,128)(2,1)S(1)}, bf16[8,32,6144]{2,1,0:T(8,128)(2,1)}, u32[]{:S(2)}) copy-start(bf16[8,32,6144]{2,1,0:T(8,128)(2,1)} %param.10) | copy-start | bytes 9437188
  20.5 6.5 copy-start.2
  20.5 6.5 copy-start.3
  20.5 6.5 copy-start.4
  20.5 76.6 %all-to-all-start.1 = ((bf16[8,2,2,16,6144]{4,3,1,0,2:T(8,128)(2,1)}), bf16[8,2,2,16,6144]{4,3,1,0,2:T(8,128)(2,1)}, u32[]{:S(2)}, u32[]{:S(2)}) async-start(bf16[8,2,2,16,6144]{4,3,1,0,2:T(8,128)(2,1)} %copy.22), calls=%async_computation.1 | async-start | bytes 12582912 | tf_op jit(solution)/shard_map/all_to_all | solution.py:60
  97.1 22.3 %all-to-all-start = ((bf16[8,4,6144]{2,1,0:T(4,128)(2,1)}), bf16[8,4,6144]{2,1,0:T(4,128)(2,1)S(1)}, u32[]{:S(2)}, u32[]{:S(2)}) async-start(bf16[8,4,6144]{2,1,0:T(4,128)(2,1)} %reshape.82), calls=%async_computation | async-start | bytes 786432 | tf_op jit(solution)/shard_map/all_to_all | solution.py:46
  119.4 143.9 %all-to-all-start.2 = ((bf16[8,2,1,32,6144]{4,3,1,2,0:T(8,128)(2,1)}), bf16[8,2,1,32,6144]{4,3,1,2,0:T(8,128)(2,1)}, u32[]{:S(2)}, u32[]{:S(2)}) async-start(bf16[8,2,1,32,6144]{4,3,1,2,0:T(8,128)(2,1)} %bitcast.42), calls=%async_computation.2 | async-start | bytes 12582912 | tf_op jit(solution)/shard_map/all_to_all | solution.py:59
  124.2 267.2 %all-gather.4.cloned.1.call-start = ((), (), s32[]{:S(2)}) async-start(), calls=%async_computation.7 | async-start | bytes 6684672 | tf_op jit(solution)/shard_map/all_gather | solution.py:76
  263.3 53.1 %all-to-all-start.3 = ((bf16[8,1,2,16,6144]{4,3,0,1,2:T(8,128)(2,1)}), bf16[8,1,2,16,6144]{4,3,0,1,2:T(8,128)(2,1)S(1)}, u32[]{:S(2)}, u32[]{:S(2)}) async-start(bf16[8,1,2,16,6144]{4,3,0,1,2:T(8,128)(2,1)} %copy.26), calls=%async_computation.3 | async-start | bytes 6291456 | tf_op jit(solution)/shard_map/all_to_all | solution.py:67
  267.2 171.5 %all-gather.6.cloned.1.call-start = ((), (), s32[]{:S(2)}) async-start(), calls=%async_computation.8 | async-start | bytes 18874368 | tf_op jit(solution)/shard_map/all_gather | solution.py:71
  273.5 248.7 %all-gather.8.cloned.1.call-start = ((), (), s32[]{:S(2)}) async-start(), calls=%async_computation.9 | async-start | bytes 9437184 | tf_op jit(solution)/shard_map/all_gather | solution.py:72
  391.3 237.4 %reduce-scatter.2.cloned.1.call-start = ((), (), s32[]{:S(2)}) async-start(), calls=%async_computation.10 | async-start | bytes 6684672 | tf_op jit(solution)/shard_map/reduce_scatter | solution.py:77
  530.4 121.5 %copy-start.1 = (bf16[8,32,6144]{2,1,0:T(8,128)(2,1)S(1)}, bf16[8,32,6144]{2,1,0:T(8,128)(2,1)}, u32[]{:S(2)}) copy-start(bf16[8,32,6144]{2,1,0:T(8,128)(2,1)} %param.10) | copy-start | bytes 9437188
Sparse Core Ops, SparseCore 0:
  127.8 68.8 all-gather.3
  273.6 165.0 all-gather.5
  440.5 81.6 all-gather.7
  530.5 98.1 reduce-scatter.1
